TPU v7x, 256 devices: a whole 4x4x8 slice. The times are simulated.
256 devices in a mesh: st: 64 (over x, z, y_lo), ta: 4 (over y_hi, core).
Axes of the slice: x: 4, y: 4 (y_hi: 2, y_lo: 2; y = y_hi * 2 + y_lo), z: 8, core: 2. Of those that a mesh axis runs over, the one named last changes fastest.
Arguments:
- samples: bfloat16 [1024, 128, 8192], P('st', 'ta'), may hold values from -6 to 6
- coefficients: float32 [16, 8192], replicated, may hold values from -1.5 to 1.5
Outputs:
- visibilities: bfloat16 [256, 2, 1024, 1024], P(('st', 'ta'))
All inputs are finite; a program needn't handle non-finite values.
Results may differ from a plain program's by a relative error of at most 0.0056.
Values may be sent and summed in bfloat16 or wider, within the bound.
A program may use at most 128 MiB of HBM per device.

v0:
```python
import math

import jax
import jax.numpy as jnp
from jax import lax
from jax.sharding import PartitionSpec as P

CH0 = 1024


def shifted(block, axis, distance):
    devices = range(lax.axis_size(axis))
    route = [(i - distance, i) for i in devices if i - distance in devices]
    return lax.ppermute(block, axis, route)


def phase_table(frame_len, channel_count, first_channel):
    positions = jnp.arange(frame_len, dtype=jnp.int32)[:, None]
    channels = (first_channel + jnp.arange(channel_count, dtype=jnp.int32))[None, :]
    phases = positions * channels % frame_len
    angles = 2.0 * math.pi / frame_len * phases.astype(jnp.float32)
    scale = jnp.float32(frame_len ** (-0.5))
    stacked = jnp.stack([jnp.cos(angles) * scale, -jnp.sin(angles) * scale], axis=2)
    return stacked.reshape(frame_len, 2 * channel_count)


def filter_frames(extended, coefficients, frame_count):
    total_sum = jnp.zeros((extended.shape[0], frame_count, extended.shape[2]), jnp.float32)
    for tap_index in range(coefficients.shape[0]):
        window = extended[:, tap_index : tap_index + frame_count, :].astype(jnp.float32)
        total_sum = total_sum + coefficients[tap_index][None, None, :] * window
    return total_sum


def channelize_rows(filtered, table):
    return jnp.einsum("ifk,kc->cif", filtered, table, precision=lax.Precision.HIGHEST)


def on_device(samples, coefficients):
    tap_count = coefficients.shape[0]
    frame_len = samples.shape[2]
    frame_count = samples.shape[1]
    st_count = lax.axis_size("st")
    ta_count = lax.axis_size("ta")
    channel_count = st_count * ta_count
    table = phase_table(frame_len, channel_count, CH0)
    head_frames = samples[:, : tap_count - 1, :]
    arrived = shifted(head_frames, "ta", -1)
    extended = jnp.concatenate([samples, arrived], 1)
    spectrum = channelize_rows(filter_frames(extended, coefficients, frame_count), table)
    spectra = spectrum.astype(jnp.bfloat16)
    turned = lax.all_to_all(
        lax.all_to_all(spectra, "st", split_axis=0, concat_axis=1, tiled=True),
        "ta",
        split_axis=0,
        concat_axis=2,
        tiled=True,
    )
    real_part = turned[0]
    imag_part = turned[1]
    all_inputs = real_part.shape[0]
    left_rows = jnp.concatenate(
        [jnp.concatenate([real_part, imag_part], 1), jnp.concatenate([imag_part, -real_part], 1)], 0
    )
    right_rows = jnp.concatenate([real_part, imag_part], 1)
    product = lax.dot_general(
        left_rows, right_rows, (((1,), (1,)), ((), ())), preferred_element_type=jnp.float32
    )
    averaged = product / jnp.float32(real_part.shape[1])
    return averaged.reshape(1, 2, all_inputs, all_inputs).astype(jnp.bfloat16)


def solution(mesh):
    return jax.shard_map(
        on_device,
        mesh=mesh,
        in_specs=(P("st", "ta", None), P()),
        out_specs=P(("st", "ta"), None, None, None),
        check_vma=False,
    )
```

profile of v0, /device:TPU:1, one launch (start us, length us, event | category | flops | bytes accessed | tf_op | source)
XLA Modules:
  0.0 257.6 jit_solution(15335294068804389901)
XLA Ops:
  0.0 2.5 slice.106
  2.5 4.2 %copy.28 = bf16[16,15,8192]{2,0,1:T(8,128)(2,1)} copy(bf16[16,15,8192]{2,1,0:T(8,128)(2,1)S(1)} %slice.106) | data formatting | bytes 7864320
  6.7 5.1 %collective-permute-start = (bf16[16,15,8192]{2,0,1:T(8,128)(2,1)}, bf16[16,15,8192]{2,0,1:T(8,128)(2,1)}, u32[]{:S(2)}, u32[]{:S(2)}) collective-permute-start(bf16[16,15,8192]{2,0,1:T(8,128)(2,1)} %copy.28), channel_id=1, source_target_pairs={{1,0},{2,1},{3,2},{5,4},{6,5},{7,6},{9,8},{10,9},{11,10},{13,12},{... | collective-permute-start | bytes 11796488 | tf_op jit(solution)/shard_map/ppermute | solution.py:14
  11.8 33.8 %cosine_multiply_fusion = (f32[8192,256,1]{1,0,2:T(8,128)S(1)}, f32[8192,256,1]{1,0,2:T(8,128)S(1)}) fusion(s32[256]{0:T(256)S(1)} %iota_add_fusion), kind=kLoop, calls=%fused_computation.89 | loop fusion | flops 35651584 | bytes 16778240 | tf_op jit(solution)/shard_map/mul | solution.py:23
  45.6 6.0 %pad_maximum_fusion = f32[8192,256,2]{1,0,2:T(8,128)} fusion(f32[8192,256,1]{1,0,2:T(8,128)S(1)} %get-tuple-element.24, f32[8192,256,1]{1,0,2:T(8,128)S(1)} %get-tuple-element.23), kind=kLoop, calls=%fused_computation | loop fusion | flops 4194304 | bytes 33554432 | tf_op jit(solution)/shard_map/stack | solution.py:23
  51.6 25.4 %copy.19 = f32[8192,256,2]{0,2,1:T(2,128)} copy(f32[8192,256,2]{1,0,2:T(8,128)} %pad_maximum_fusion) | data formatting | bytes 33554432 | tf_op jit(solution)/shard_map/stack | solution.py:23
  77.0 20.5 %reshape.147 = f32[8192,512]{0,1:T(8,128)} reshape(f32[8192,256,2]{0,2,1:T(2,128)} %copy.19) | data formatting | bytes 33554432 | tf_op jit(solution)/shard_map/reshape | solution.py:24
  97.5 0.0 copy-start
  97.5 7.7 %constant_dynamic-update-slice_fusion = bf16[16,47,8192]{2,1,0:T(8,128)(2,1)} fusion(bf16[16,32,8192]{2,1,0:T(8,128)(2,1)} %param.2), kind=kLoop, calls=%fused_computation.105 | loop fusion | bytes 16777216
  105.2 0.0 copy-done
  105.2 0.5 fusion.103
  105.7 0.0 collective-permute-done
  105.7 6.3 %copy_dynamic-update-slice_fusion = bf16[16,47,8192]{2,1,0:T(8,128)(2,1)} fusion(bf16[16,47,8192]{2,1,0:T(8,128)(2,1)} %constant_dynamic-update-slice_fusion, bf16[16,15,8192]{2,0,1:T(8,128)(2,1)} %collective-permute-done), kind=kLoop, calls=%fused_computation.93 | loop fusion | bytes 8126464 | tf_op jit(solution)/shard_map/concatenate | solution.py:49
  112.0 89.8 %fusion.86 = bf16[512,16,32]{0,2,1:T(8,128)(2,1)S(1)} fusion(bf16[16,32,8192]{2,1,0:T(8,128)(2,1)} %param.2, bf16[16,47,8192]{2,1,0:T(8,128)(2,1)} %copy_dynamic-update-slice_fusion, f32[8192]{0:T(1024)S(1)} %bitcast.54, f32[8192]{0:T(1024)S(1)} %bitcast.55, f32[8192]{0:T(1024)S(1)} %bitcast.41, f32[8192]{0:T(1024)S(1)} %bitcast.42, f32[8192]{0:T(1024)S(1)} %bitcast.43, ...), kind=kOutput, calls=%fused_computation.94 | convolution fusion | flops 25967198208 | bytes 152043520 | tf_op jit(solution)/shard_map/ifk,kc->cif/dot_general | solution.py:36
  201.7 2.0 copy.23
  203.7 2.1 reshape.149
  205.8 28.5 %all_to_all.33 = bf16[64,2,2048]{2,1,0:T(2,128)(2,1)S(1)} all-to-all(bf16[64,2,2048]{2,1,0:T(2,128)(2,1)S(1)} %reshape.149), channel_id=1, replica_groups=mesh['st'=64,'ta'=4] {'st'}, dimensions={0} | all-to-all | bytes 1048576 | tf_op jit(solution)/shard_map/all_to_all | solution.py:53
  234.3 1.0 reshape.150
  235.3 1.7 copy.24
  237.0 1.9 copy.25
  238.9 15.2 %all_to_all.34 = bf16[8,1024,32]{1,2,0:T(8,128)(2,1)S(1)} all-to-all(bf16[8,1024,32]{1,2,0:T(8,128)(2,1)S(1)} %copy.25), channel_id=1, replica_groups=mesh['st'=64,'ta'=4] {'ta'}, dimensions={0} | all-to-all | bytes 1048576 | tf_op jit(solution)/shard_map/all_to_all | solution.py:52
  254.2 3.3 %multiply_convert_fusion = bf16[2048,1024]{1,0:T(8,128)(2,1)} fusion(bf16[1024,128]{0,1:T(8,128)(2,1)S(1)} %bitcast_negate_fusion, bf16[1024,128]{0,1:T(8,128)(2,1)S(1)} %bitcast.39, bf16[1024,128]{0,1:T(8,128)(2,1)S(1)} %bitcast.38), kind=kOutput, calls=%fused_computation.71 | convolution fusion | flops 1083179008 | bytes 4980736 | tf_op jit(solution)/shard_map/dot_general | solution.py:66
  (3 shorter events, 0.1 us)
Async XLA Ops:
  6.7 99.0 %collective-permute-start = (bf16[16,15,8192]{2,0,1:T(8,128)(2,1)}, bf16[16,15,8192]{2,0,1:T(8,128)(2,1)}, u32[]{:S(2)}, u32[]{:S(2)}) collective-permute-start(bf16[16,15,8192]{2,0,1:T(8,128)(2,1)} %copy.28), channel_id=1, source_target_pairs={{1,0},{2,1},{3,2},{5,4},{6,5},{7,6},{9,8},{10,9},{11,10},{13,12},{... | collective-permute-start | bytes 11796488 | tf_op jit(solution)/shard_map/ppermute | solution.py:14
  97.5 7.7 %copy-start = (f32[16,8192]{1,0:T(8,128)S(1)}, f32[16,8192]{1,0:T(8,128)}, u32[]{:S(2)}) copy-start(f32[16,8192]{1,0:T(8,128)} %param.3) | copy-start | bytes 1572868
where the time goes:
time: 262 us; the launch traced here: 258 us
  matrix products  93.1 us (36%)
  local copies, waits for them, and re-layouts  75.7 us (29%)
  blocking collectives  43.7 us (17%)
  other arithmetic  39.8 us (15%)
  starting transfers between devices  5.1 us (2%)
    dot_general x1, matrix products, channelize_rows(): jnp.einsum('ifk,kc->cif', filtered, table, precision=lax.Precision.HIGHEST)  89.8 us
    mul x1, other arithmetic, phase_table(): jnp.cos(angles) * scale  33.8 us
    all_to_all x1, blocking collectives, on_device(): lax.all_to_all(spectra, 'st', split_axis=0, concat_axis=1, tiled=True)  28.5 us
    another operation x1, local copies, waits for them, and re-layouts, phase_table(): jnp.stack([jnp.cos(angles) * scale, -jnp.sin(angles) * scale], axis=2)  25.4 us
    reshape x1, local copies, waits for them, and re-layouts, phase_table(): return stacked.reshape(frame_len, 2 * channel_count)  20.5 us
    all_to_all x1, blocking collectives, on_device(): lax.all_to_all(lax.all_to_all(spectra, 'st', split_axis=0, concat_axis=1,...  15.2 us
    unnamed x6, local copies, waits for them, and re-layouts  15 us
    concatenate x1, local copies, waits for them, and re-layouts, on_device(): extended = jnp.concatenate([samples, arrived], 1)  6.27 us
  transfers between devices with their start and end apart: 1, of which 0 were waited for; matrix products, arithmetic and copies ran while one was open for 36% of the time, Pallas kernels for 0%

commit v1 on v0

v1 whole, which is shorter than its diff:
```python
import functools
import math

import jax
import jax.numpy as jnp
import numpy as np
from jax import lax
from jax.experimental import pallas as pl
from jax.experimental.pallas import tpu as pltpu
from jax.sharding import PartitionSpec as P

CH0 = 1024
MESH_IDS = pl.DeviceIdType.MESH
BF16 = jnp.bfloat16
F32 = jnp.float32

NFFT = 8192
TAPS = 16
INPUTS_HERE = 16
FRAMES_HERE = 32
CHANNELS = 256
BINS = 24
HALF = 8
QUARTER = NFFT // 4
CHUNK = 256
STEPS = QUARTER // CHUNK


def _as_bf16(values):
    return np.asarray(values, np.float32).astype(BF16)


def _high_low(values):
    high = _as_bf16(values)
    return high, _as_bf16(values - high.astype(np.float64))


def _bin_angles():
    return 2.0 * np.pi * (np.arange(BINS) + 0.5) / (2 * BINS)


def _forward_matrix():
    angles = _bin_angles()[:, None] * np.arange(FRAMES_HERE)[None, :]
    parts = np.stack([np.cos(angles), -np.sin(angles)])
    block = np.zeros((2, HALF, BINS, HALF, FRAMES_HERE))
    for i in range(HALF):
        block[:, i, :, i, :] = parts
    return block.reshape(2 * HALF * BINS, HALF * FRAMES_HERE)


def _tap_matrix():
    angles = _bin_angles()[:, None] * np.arange(TAPS)[None, :]
    taps = np.concatenate([np.cos(angles), np.sin(angles)])
    high, low = _high_low(taps)
    return np.concatenate([high, high, low], 1)


def _inverse_matrices():
    scale = (2.0 / (2 * BINS)) * NFFT ** -0.5
    frames = np.arange(FRAMES_HERE)
    angles = _bin_angles()[:, None] * frames[None, :]
    own = scale * np.stack([np.cos(angles), -np.sin(angles)])
    before = _bin_angles()[:, None] * (frames - FRAMES_HERE)[None, :]
    halo = scale * np.stack([np.cos(before), -np.sin(before)])
    halo[:, :, : FRAMES_HERE - (TAPS - 1)] = 0.0
    out = []
    for parity in range(2):
        placed = halo if parity == 0 else np.roll(halo, -FRAMES_HERE // 2, axis=2)
        rows = np.zeros((2, 2, 2, FRAMES_HERE, 2, 2, 2, BINS))
        for p in range(2):
            for ri in range(2):
                rows[0, p, ri, :, ri, p] = np.moveaxis(own, 2, 0)
                rows[1, p, ri, :, ri, p] = np.moveaxis(placed, 2, 0)
        high, low = _high_low(rows.reshape(8 * FRAMES_HERE, 8 * BINS))
        out.append(np.concatenate([high, high, low], 1))
    return np.stack(out)


def _channel_table():
    positions = np.arange(QUARTER)[:, None]
    columns = []
    for odd in range(2):
        channels = CH0 + np.arange(odd, CHANNELS, 2)[None, :]
        angles = 2.0 * np.pi * (positions * channels % NFFT) / NFFT
        columns += [np.cos(angles), -np.sin(angles)]
    return _as_bf16(np.concatenate(columns, 1))


def _turn_signs():
    even = np.where(np.arange(0, CHANNELS, 2) % 4 == 0, 1.0, -1.0)
    odd = np.where(np.arange(1, CHANNELS, 2) % 4 == 1, 1.0, -1.0)
    rows = np.concatenate([even, even, odd, -odd])[None, :]
    return _as_bf16(np.broadcast_to(rows, (16, 2 * CHANNELS)))


def _dot(a, b):
    return jnp.dot(a, b, preferred_element_type=F32)


def _split(values):
    high = values.astype(BF16)
    return high, (values - high.astype(F32)).astype(BF16)


def channelize_kernel(x0, x1, x2, x3, c0, c1, c2, c3, table, signs, forward, taps, inverse, own, halo, acc):
    step = pl.program_id(0)

    @pl.when(step == 0)
    def _():
        acc[...] = jnp.zeros_like(acc)

    tap_matrix = taps[...]
    responses = []
    for coefficient in (c0, c1, c2, c3):
        high, low = _split(coefficient[...])
        response = _dot(tap_matrix, jnp.concatenate([high, low, high], 0))
        responses.append((response[:BINS][None], response[BINS:][None]))
    table_even = table[:, : CHANNELS]
    table_odd = table[:, CHANNELS :]
    half = CHANNELS // 2
    turned_even = table_even * signs[0:1, : CHANNELS]
    turned_odd = jnp.concatenate([table_odd[:, half:], table_odd[:, :half]], 1) * signs[0:1, CHANNELS :]
    matrix = forward[...]
    rows = HALF * FRAMES_HERE
    for h in range(2):
        products = []
        for x, (real, imag) in zip((x0, x1, x2, x3), responses):
            z = _dot(matrix, x[h * rows : (h + 1) * rows, :])
            zr = z[: HALF * BINS].reshape(HALF, BINS, CHUNK)
            zi = z[HALF * BINS :].reshape(HALF, BINS, CHUNK)
            yr = (zr * real - zi * imag).reshape(HALF * BINS, CHUNK)
            yi = (zr * imag + zi * real).reshape(HALF * BINS, CHUNK)
            products.append((yr, yi))
        (r0, i0), (r1, i1), (r2, i2), (r3, i3) = products
        even0 = jnp.concatenate([(r0 + r2).astype(BF16), (i0 + i2).astype(BF16)], 0)
        odd0 = jnp.concatenate([(r0 - r2).astype(BF16), (i0 - i2).astype(BF16)], 0)
        even1 = jnp.concatenate([(r1 + r3).astype(BF16), (i1 + i3).astype(BF16)], 0)
        odd1 = jnp.concatenate([(r1 - r3).astype(BF16), (i1 - i3).astype(BF16)], 0)
        acc[h, :, : CHANNELS] += _dot(even0, table_even) + _dot(even1, turned_even)
        acc[h, :, CHANNELS :] += _dot(odd0, table_odd) + _dot(odd1, turned_odd)

    @pl.when(step == STEPS - 1)
    def _():
        held = None
        for s in (0, 4, 1, 5, 2, 6, 3, 7):
            pieces = []
            for ri in range(2):
                for p in range(2):
                    for part in range(2):
                        start = part * HALF * BINS + s * BINS
                        block = acc[p, start : start + BINS, :]
                        left = ri * half
                        pieces.append(
                            jnp.concatenate(
                                [block[:, left : left + half], block[:, CHANNELS + left : CHANNELS + left + half]], 1
                            )
                        )
            stacked = jnp.concatenate(pieces, 0)
            high, low = _split(stacked)
            result = _dot(inverse[s // 4], jnp.concatenate([high, low, high], 0))
            mine, before = result[:128], result[128:]
            own[pl.ds(s, half, stride=2 * HALF), :] = mine[:, :half].T
            own[pl.ds(HALF + s, half, stride=2 * HALF), :] = mine[:, half:].T
            if s < HALF // 2:
                held = before
            else:
                both = held + before
                j = s - HALF // 2
                halo[pl.ds(j, half, stride=HALF), :] = both[:, :half].T
                halo[pl.ds(HALF // 2 + j, half, stride=HALF), :] = both[:, half:].T


def channelize(samples, coefficients):
    x = samples.reshape(INPUTS_HERE * FRAMES_HERE, NFFT)
    whole = lambda *shape: pl.BlockSpec(shape, lambda j: (0,) * len(shape))
    x_specs = [
        pl.BlockSpec((INPUTS_HERE * FRAMES_HERE, CHUNK), functools.partial(lambda q, j: (0, q * STEPS + j), q))
        for q in range(4)
    ]
    c_specs = [
        pl.BlockSpec((TAPS, CHUNK), functools.partial(lambda q, j: (0, q * STEPS + j), q)) for q in range(4)
    ]
    table, signs = _channel_table(), _turn_signs()
    forward, taps, inverse = _as_bf16(_forward_matrix()), _tap_matrix(), _inverse_matrices()
    return pl.pallas_call(
        channelize_kernel,
        out_shape=(
            jax.ShapeDtypeStruct((CHANNELS * HALF, 128), F32),
            jax.ShapeDtypeStruct((CHANNELS * HALF // 2, 128), F32),
        ),
        grid=(STEPS,),
        in_specs=x_specs
        + c_specs
        + [
            pl.BlockSpec((CHUNK, 2 * CHANNELS), lambda j: (j, 0)),
            whole(*signs.shape),
            whole(*forward.shape),
            whole(*taps.shape),
            whole(*inverse.shape),
        ],
        out_specs=(whole(CHANNELS * HALF, 128), whole(CHANNELS * HALF // 2, 128)),
        scratch_shapes=[pltpu.VMEM((2, 2 * HALF * BINS, 2 * CHANNELS), F32)],
        name="channelize",
    )(x, x, x, x, coefficients, coefficients, coefficients, coefficients, table, signs, forward, taps, inverse)


def exchange_kernel(
    own, halo, out, message, total, leaving, arrived, wide, local_sem, halo_send, halo_recv, send_sem, recv_sem
):
    st = lax.axis_index("st")
    ta = lax.axis_index("ta")
    ta_count = 4
    count = CHANNELS
    me = st * ta_count + ta
    barrier = pltpu.get_barrier_semaphore()

    def greet(d, carry):
        peer = lax.rem(me + d, count)
        pl.semaphore_signal(
            barrier, inc=1, device_id=(peer // ta_count, lax.rem(peer, ta_count)), device_id_type=MESH_IDS
        )
        return carry

    lax.fori_loop(1, count, greet, 0)
    leaving[...] = halo[...].astype(BF16)
    pl.semaphore_wait(barrier, count - 1)

    def halo_copy(target):
        return pltpu.make_async_remote_copy(
            src_ref=leaving, dst_ref=arrived, send_sem=halo_send, recv_sem=halo_recv,
            device_id=(st, target), device_id_type=MESH_IDS,
        )

    @pl.when(ta > 0)
    def _():
        halo_copy(ta - 1).start()

    @pl.when(ta == ta_count - 1)
    def _():
        message[...] = own[...].reshape(CHANNELS, HALF, 128).astype(BF16)

    @pl.when(ta < ta_count - 1)
    def _():
        halo_copy(ta).wait_recv()
        wide[...] = arrived[...].astype(F32)
        lane = lax.broadcasted_iota(jnp.int32, (CHANNELS, 128), 1)
        late = lax.rem(lane, FRAMES_HERE) >= FRAMES_HERE // 2
        for s in range(HALF):
            packed = wide[pl.ds(s % 4, CHANNELS, stride=4), :]
            if s >= HALF // 2:
                packed = pltpu.roll(packed, FRAMES_HERE // 2, 1)
            rows = pl.ds(s, CHANNELS, stride=HALF)
            total[rows, :] = own[rows, :] + jnp.where(late, packed, 0.0)
        message[...] = total[...].reshape(CHANNELS, HALF, 128).astype(BF16)

    keep = pltpu.make_async_copy(message.at[me], out.at[me], local_sem)
    keep.start()

    def send(d, carry):
        peer = lax.rem(me + d, count)
        pltpu.make_async_remote_copy(
            src_ref=message.at[peer], dst_ref=out.at[me], send_sem=send_sem, recv_sem=recv_sem,
            device_id=(peer // ta_count, lax.rem(peer, ta_count)), device_id_type=MESH_IDS,
        ).start()
        return carry

    lax.fori_loop(1, count, send, 0)
    keep.wait()

    @pl.when(ta > 0)
    def _():
        halo_copy(ta - 1).wait_send()

    pltpu.make_async_remote_copy(
        src_ref=message.at[pl.ds(0, count - 1)], dst_ref=out.at[pl.ds(0, count - 1)], send_sem=send_sem,
        recv_sem=recv_sem, device_id=(st, ta), device_id_type=MESH_IDS,
    ).wait()


def exchange(own, halo):
    vmem = pl.BlockSpec(memory_space=pltpu.VMEM)
    return pl.pallas_call(
        exchange_kernel,
        out_shape=jax.ShapeDtypeStruct((CHANNELS, HALF, 128), BF16),
        in_specs=[vmem, vmem],
        out_specs=vmem,
        scratch_shapes=[
            pltpu.VMEM((CHANNELS, HALF, 128), BF16),
            pltpu.VMEM((CHANNELS * HALF, 128), F32),
            pltpu.VMEM((CHANNELS * HALF // 2, 128), BF16),
            pltpu.VMEM((CHANNELS * HALF // 2, 128), BF16),
            pltpu.VMEM((CHANNELS * HALF // 2, 128), F32),
        ]
        + [pltpu.SemaphoreType.DMA] * 5,
        compiler_params=pltpu.CompilerParams(collective_id=0, has_side_effects=True),
        name="exchange",
    )(own, halo)


ROWS = 256


def correlate_kernel(arrived, out, spectra):
    inputs = spectra.shape[0]
    step = pl.program_id(0)

    @pl.when(step == 0)
    def _():
        lane = lax.broadcasted_iota(jnp.int32, (8, 8, 128), 2) // FRAMES_HERE

        def place(b, carry):
            tiles = arrived[pl.ds(b * 32, 32)].astype(F32).reshape(8, 4, 8, 128)
            for p in range(2):
                for ri in range(2):
                    g = 2 * p + ri
                    made = None
                    for ta in range(4):
                        turned = tiles[:, ta]
                        if ta != g:
                            turned = pltpu.roll(turned, (ta - g) % 4 * FRAMES_HERE, 2)
                        made = turned if made is None else jnp.where(lane == ta, turned, made)
                    for k in range(8):
                        start = pl.multiple_of(b * 128 + k * 16 + p * 8, 8)
                        wide_rows = made[k]
                        spectra[pl.ds(start, 8), ri * 128 : (ri + 1) * 128] = wide_rows
            return carry

        lax.fori_loop(0, inputs // 128, place, 0)

    start = pl.multiple_of(step * ROWS, ROWS)
    block = spectra[pl.ds(start, ROWS), :].astype(BF16)
    everything = spectra[...].astype(BF16)
    contract = (((1,), (1,)), ((), ()))
    swapped = jnp.concatenate([block[:, 128:], -block[:, :128]], 1)
    scale = 1.0 / 128
    out[0, 0] = (lax.dot_general(block, everything, contract, preferred_element_type=F32) * scale).astype(BF16)
    out[0, 1] = (lax.dot_general(swapped, everything, contract, preferred_element_type=F32) * scale).astype(BF16)


def correlate(arrived):
    inputs = arrived.shape[0] // 4 * INPUTS_HERE
    return pl.pallas_call(
        correlate_kernel,
        out_shape=jax.ShapeDtypeStruct((1, 2, inputs, inputs), BF16),
        grid=(inputs // ROWS,),
        in_specs=[pl.BlockSpec(arrived.shape, lambda i: (0, 0, 0))],
        out_specs=pl.BlockSpec((1, 2, ROWS, inputs), lambda i: (0, 0, i, 0)),
        scratch_shapes=[pltpu.VMEM((inputs, 256), F32)],
        name="correlate",
    )(arrived)


def on_device(samples, coefficients):
    own, halo = channelize(samples, coefficients)
    return correlate(exchange(own, halo))


def solution(mesh):
    return jax.shard_map(
        on_device,
        mesh=mesh,
        in_specs=(P("st", "ta", None), P()),
        out_specs=P(("st", "ta"), None, None, None),
        check_vma=False,
    )
```

time: 262 us -> 56.1 us (0.21); the launches traced: 258 us -> 55.9 us
  matrix products: 93.1 us -> 0 us
  local copies, waits for them, and re-layouts: 75.7 us -> 0 us
  Pallas kernels: 0 us -> 55.9 us
  blocking collectives: 43.7 us -> 0 us
  other arithmetic: 39.8 us -> 0 us
  starting transfers between devices: 5.1 us -> 0 us
    dot_general x2 -> x0, matrix products: 93.1 us -> none  [the longest x1 89.8 us: channelize_rows(): jnp.einsum('ifk,kc->cif', filtered, table, precision=lax.Precision.HIGHEST)]
    pallas_call x0 -> x3, Pallas kernels: none -> 55.9 us  [the longest x1 34.4 us: exchange(): pl.pallas_call(exchange_kernel, out_shape=jax.ShapeDtypeStruct((CHANNELS,...]
    all_to_all x2 -> x0, blocking collectives: 43.7 us -> none  [the longest x1 28.5 us: on_device(): lax.all_to_all(spectra, 'st', split_axis=0, concat_axis=1, tiled=True)]
    mul x1 -> x0, other arithmetic: 33.8 us -> none  [phase_table(): jnp.cos(angles) * scale]
    another operation x1 -> x0, local copies, waits for them, and re-layouts: 25.4 us -> none  [phase_table(): jnp.stack([jnp.cos(angles) * scale, -jnp.sin(angles) * scale], axis=2)]
    reshape x1 -> x0, local copies, waits for them, and re-layouts: 20.5 us -> none  [phase_table(): return stacked.reshape(frame_len, 2 * channel_count)]
    unnamed x6 -> x0, local copies, waits for them, and re-layouts: 15 us -> none
    concatenate x1 -> x0, local copies, waits for them, and re-layouts: 6.27 us -> none  [on_device(): extended = jnp.concatenate([samples, arrived], 1)]
  transfers between devices with their start and end apart: 1 -> 0, of which waited for: 0 -> 0; matrix products, arithmetic and copies ran while one was open for 36% -> 0% of each run, Pallas kernels for 0% -> 0%
where the time goes in v1:
time: 56.1 us; the launch traced here: 55.9 us
  Pallas kernels  55.9 us (100%)
    pallas_call x1, Pallas kernels, exchange(): pl.pallas_call(exchange_kernel, out_shape=jax.ShapeDtypeStruct((CHANNELS,...  34.4 us
    pallas_call x1, Pallas kernels, channelize(): pl.pallas_call(channelize_kernel, out_shape=(jax.ShapeDtypeStruct((CHANNE...  16.1 us
    pallas_call x1, Pallas kernels, correlate(): pl.pallas_call(correlate_kernel, out_shape=jax.ShapeDtypeStruct((1, 2, in...  5.45 us

profile of v1, /device:TPU:1, one launch (start us, length us, event | category | flops | bytes accessed | tf_op | source)
XLA Modules:
  0.0 55.9 jit_solution(9619465817200477534)
XLA Ops:
  0.0 16.1 %channelize.1 = (f32[2048,128]{1,0:T(8,128)}, f32[1024,128]{1,0:T(8,128)}) custom-call(bf16[512,8192]{1,0:T(8,128)(2,1)} %bitcast.1, bf16[512,8192]{1,0:T(8,128)(2,1)} %bitcast.2, bf16[512,8192]{1,0:T(8,128)(2,1)} %bitcast.3, bf16[512,8192]{1,0:T(8,128)(2,1)} %bitcast.4, f32[16,8192]{1,0:T(8,128)} %c3.1, f32[16,8192]{1,0:T(8,128)} %c3.1, f32[16,8192]{1,0:T(8,128)} %c3.1, ...), custom_call_target="tpu_custom_call" | custom-call | tf_op jit(solution)/shard_map/channelize/pallas_call | solution.py:185
  16.1 34.4 %exchange.1.arrived = bf16[256,8,128]{2,1,0:T(8,128)(2,1)} custom-call(f32[2048,128]{1,0:T(8,128)} %get-tuple-element.7.own, f32[1024,128]{1,0:T(8,128)} %get-tuple-element.8.halo), custom_call_target="tpu_custom_call" | custom-call | tf_op jit(solution)/shard_map/exchange/pallas_call | solution.py:282
  50.5 5.5 %correlate.1 = bf16[1,2,1024,1024]{3,2,1,0:T(8,128)(2,1)} custom-call(bf16[256,8,128]{2,1,0:T(8,128)(2,1)} %exchange.1.arrived), custom_call_target="tpu_custom_call" | custom-call | tf_op jit(solution)/shard_map/correlate/pallas_call | solution.py:342

commit v2 on v1

v2 whole, which is shorter than its diff:
```python
import functools
import math

import jax
import jax.numpy as jnp
import numpy as np
from jax import lax
from jax.experimental import pallas as pl
from jax.experimental.pallas import tpu as pltpu
from jax.sharding import PartitionSpec as P

CH0 = 1024
LOGICAL = pl.DeviceIdType.LOGICAL
BF16 = jnp.bfloat16
F32 = jnp.float32

NFFT = 8192
TAPS = 16
INPUTS_HERE = 16
FRAMES_HERE = 32
CHANNELS = 256
TA = 4
BINS = 24
HALF = 8
GROUPS = 4
HALF_FRAMES = FRAMES_HERE // 2
QUARTER = NFFT // 4
CHUNK = 256
STEPS = QUARTER // CHUNK


def _as_bf16(values):
    return np.asarray(values, np.float32).astype(BF16)


def _high_low(values):
    high = _as_bf16(values)
    return high, _as_bf16(values - high.astype(np.float64))


def _bin_angles():
    return 2.0 * np.pi * (np.arange(BINS) + 0.5) / (2 * BINS)


def _forward_matrix():
    angles = _bin_angles()[:, None] * np.arange(FRAMES_HERE)[None, :]
    parts = np.stack([np.cos(angles), -np.sin(angles)])
    block = np.zeros((2, HALF, BINS, HALF, FRAMES_HERE))
    for i in range(HALF):
        block[:, i, :, i, :] = parts
    return block.reshape(2 * HALF * BINS, HALF * FRAMES_HERE)


def _tap_matrix():
    angles = _bin_angles()[:, None] * np.arange(TAPS)[None, :]
    taps = np.concatenate([np.cos(angles), np.sin(angles)])
    high, low = _high_low(taps)
    return np.concatenate([high, high, low], 1)


def _inverse_matrix():
    scale = (2.0 / (2 * BINS)) * NFFT ** -0.5
    rows = np.zeros((3, GROUPS, 2, HALF_FRAMES, 2, GROUPS, 2, BINS))
    for kind, first in enumerate((0, HALF_FRAMES, -HALF_FRAMES)):
        frames = first + np.arange(HALF_FRAMES)
        angles = _bin_angles()[:, None] * frames[None, :]
        values = scale * np.stack([np.cos(angles), -np.sin(angles)])
        if first < 0:
            values[:, :, frames <= -TAPS] = 0.0
        for p in range(GROUPS):
            for ri in range(2):
                rows[kind, p, ri, :, ri, p] = np.moveaxis(values, 2, 0)
    high, low = _high_low(rows.reshape(3 * 128, 4 * GROUPS * BINS))
    return np.concatenate([high, high, low], 1)


def _channel_table():
    positions = np.arange(QUARTER)[:, None]
    columns = []
    for odd in range(2):
        channels = CH0 + np.arange(odd, CHANNELS, 2)[None, :]
        angles = 2.0 * np.pi * (positions * channels % NFFT) / NFFT
        columns += [np.cos(angles), -np.sin(angles)]
    return _as_bf16(np.concatenate(columns, 1))


def _turn_signs():
    even = np.where(np.arange(0, CHANNELS, 2) % 4 == 0, 1.0, -1.0)
    odd = np.where(np.arange(1, CHANNELS, 2) % 4 == 1, 1.0, -1.0)
    rows = np.concatenate([even, even, odd, -odd])[None, :]
    return _as_bf16(np.broadcast_to(rows, (16, 2 * CHANNELS)))


def _dot(a, b):
    return jnp.dot(a, b, preferred_element_type=F32)


def _split(values):
    high = values.astype(BF16)
    return high, (values - high.astype(F32)).astype(BF16)


def spectra_kernel(
    x0, x1, x2, x3, c0, c1, c2, c3, table, signs, forward, taps, inverse,
    out,
    acc, own, halo, early, late, leaving, arrived, wide, local_sem, halo_send, halo_recv, send_sem, recv_sem,
):
    step = pl.program_id(0)
    st = lax.axis_index("st")
    ta = lax.axis_index("ta")
    me = st * TA + ta
    barrier = pltpu.get_barrier_semaphore()

    def over_others(body):
        def run(peer, carry):
            body(peer)
            return carry

        lax.fori_loop(me + 1, CHANNELS, run, 0)
        lax.fori_loop(0, me, run, 0)

    @pl.when(step == 0)
    def _():
        over_others(lambda peer: pl.semaphore_signal(barrier, inc=1, device_id=peer, device_id_type=LOGICAL))
        acc[...] = jnp.zeros_like(acc)

    tap_matrix = taps[...]
    responses = []
    for coefficient in (c0, c1, c2, c3):
        high, low = _split(coefficient[...])
        response = _dot(tap_matrix, jnp.concatenate([high, low, high], 0))
        responses.append((response[:BINS][None], response[BINS:][None]))
    table_even = table[:, : CHANNELS]
    table_odd = table[:, CHANNELS :]
    half = CHANNELS // 2
    turned_even = table_even * signs[0:1, : CHANNELS]
    turned_odd = jnp.concatenate([table_odd[:, half:], table_odd[:, :half]], 1) * signs[0:1, CHANNELS :]
    matrix = forward[...]
    rows = HALF * FRAMES_HERE
    for h in range(2):
        products = []
        for x, (real, imag) in zip((x0, x1, x2, x3), responses):
            z = _dot(matrix, x[h * rows : (h + 1) * rows, :])
            zr = z[: HALF * BINS].reshape(HALF, BINS, CHUNK)
            zi = z[HALF * BINS :].reshape(HALF, BINS, CHUNK)
            yr = (zr * real - zi * imag).reshape(HALF * BINS, CHUNK)
            yi = (zr * imag + zi * real).reshape(HALF * BINS, CHUNK)
            products.append((yr, yi))
        (r0, i0), (r1, i1), (r2, i2), (r3, i3) = products
        even0 = jnp.concatenate([(r0 + r2).astype(BF16), (i0 + i2).astype(BF16)], 0)
        odd0 = jnp.concatenate([(r0 - r2).astype(BF16), (i0 - i2).astype(BF16)], 0)
        even1 = jnp.concatenate([(r1 + r3).astype(BF16), (i1 + i3).astype(BF16)], 0)
        odd1 = jnp.concatenate([(r1 - r3).astype(BF16), (i1 - i3).astype(BF16)], 0)
        acc[h, :, : CHANNELS] += _dot(even0, table_even) + _dot(even1, turned_even)
        acc[h, :, CHANNELS :] += _dot(odd0, table_odd) + _dot(odd1, turned_odd)

    def transform_back():
        for s in range(HALF // 2):
            pieces = []
            for ri in range(2):
                left = ri * half
                for p in range(GROUPS):
                    for part in range(2):
                        start = part * HALF * BINS + (p % 2 * 4 + s) * BINS
                        block = acc[p // 2, start : start + BINS, :]
                        pieces.append(
                            jnp.concatenate(
                                [block[:, left : left + half], block[:, CHANNELS + left : CHANNELS + left + half]], 1
                            )
                        )
            high, low = _split(jnp.concatenate(pieces, 0))
            result = _dot(inverse[...], jnp.concatenate([high, low, high], 0))
            for odd in range(2):
                columns = slice(odd * half, (odd + 1) * half)
                own[pl.ds(odd * 8 + s, half, stride=16), :] = result[:128, columns].T
                own[pl.ds(odd * 8 + 4 + s, half, stride=16), :] = result[128:256, columns].T
                halo[pl.ds(odd * 4 + s, half, stride=8), :] = result[256:, columns].T

    def halo_copy(target):
        return pltpu.make_async_remote_copy(
            src_ref=leaving, dst_ref=arrived, send_sem=halo_send, recv_sem=halo_recv,
            device_id=st * TA + target, device_id_type=LOGICAL,
        )

    def part_copies(message, first):
        rows = pl.ds(first, 4)

        def send(peer):
            pltpu.make_async_remote_copy(
                src_ref=message.at[peer, rows], dst_ref=out.at[me, rows], send_sem=send_sem, recv_sem=recv_sem,
                device_id=peer, device_id_type=LOGICAL,
            ).start()

        keep = pltpu.make_async_copy(message.at[me, rows], out.at[me, rows], local_sem.at[first // 4])
        keep.start()
        over_others(send)
        return keep

    @pl.when(step == STEPS - 1)
    def _():
        transform_back()
        leaving[...] = halo[...].astype(BF16)
        early[...] = own[...].reshape(CHANNELS, HALF, 128).astype(BF16)
        pl.semaphore_wait(barrier, CHANNELS - 1)

        @pl.when(ta > 0)
        def _():
            halo_copy(ta - 1).start()

        keep_early = part_copies(early, 0)

        @pl.when(ta < TA - 1)
        def _():
            halo_copy(ta).wait_recv()
            wide[...] = arrived[...].astype(F32)
            for s in range(4):
                rows = pl.ds(4 + s, CHANNELS, stride=HALF)
                own[rows, :] += wide[pl.ds(s, CHANNELS, stride=4), :]

        late[...] = own[...].reshape(CHANNELS, HALF, 128).astype(BF16)
        keep_late = part_copies(late, 4)
        keep_early.wait()
        keep_late.wait()

        @pl.when(ta > 0)
        def _():
            halo_copy(ta - 1).wait_send()

        everything = pl.ds(0, CHANNELS - 1)
        pltpu.make_async_remote_copy(
            src_ref=late.at[everything], dst_ref=out.at[everything], send_sem=send_sem, recv_sem=recv_sem,
            device_id=me, device_id_type=LOGICAL,
        ).wait()


def gather_spectra(samples, coefficients):
    x = samples.reshape(INPUTS_HERE * FRAMES_HERE, NFFT)
    whole = lambda *shape: pl.BlockSpec(shape, lambda j: (0,) * len(shape))
    x_specs = [
        pl.BlockSpec((INPUTS_HERE * FRAMES_HERE, CHUNK), functools.partial(lambda q, j: (0, q * STEPS + j), q))
        for q in range(4)
    ]
    c_specs = [
        pl.BlockSpec((TAPS, CHUNK), functools.partial(lambda q, j: (0, q * STEPS + j), q)) for q in range(4)
    ]
    table, signs = _channel_table(), _turn_signs()
    forward, taps, inverse = _as_bf16(_forward_matrix()), _tap_matrix(), _inverse_matrix()
    rows = CHANNELS * HALF
    return pl.pallas_call(
        spectra_kernel,
        out_shape=jax.ShapeDtypeStruct((CHANNELS, HALF, 128), BF16),
        grid=(STEPS,),
        in_specs=x_specs
        + c_specs
        + [
            pl.BlockSpec((CHUNK, 2 * CHANNELS), lambda j: (j, 0)),
            whole(*signs.shape),
            whole(*forward.shape),
            whole(*taps.shape),
            whole(*inverse.shape),
        ],
        out_specs=pl.BlockSpec(memory_space=pl.ANY),
        scratch_shapes=[
            pltpu.VMEM((2, 2 * HALF * BINS, 2 * CHANNELS), F32),
            pltpu.VMEM((rows, 128), F32),
            pltpu.VMEM((rows // 2, 128), F32),
            pltpu.VMEM((CHANNELS, HALF, 128), BF16),
            pltpu.VMEM((CHANNELS, HALF, 128), BF16),
            pltpu.VMEM((rows // 2, 128), BF16),
            pltpu.VMEM((rows // 2, 128), BF16),
            pltpu.VMEM((rows // 2, 128), F32),
            pltpu.SemaphoreType.DMA((2,)),
        ]
        + [pltpu.SemaphoreType.DMA] * 4,
        compiler_params=pltpu.CompilerParams(collective_id=0, has_side_effects=True),
        name="spectra",
    )(x, x, x, x, coefficients, coefficients, coefficients, coefficients, table, signs, forward, taps, inverse)


ROWS = 256


def correlate_kernel(arrived, out, spectra, wide):
    inputs = spectra.shape[1]
    step = pl.program_id(0)

    @pl.when(step == 0)
    def _():
        wide[...] = arrived[...].astype(F32).reshape(wide.shape)
        sources = inputs // INPUTS_HERE
        lane = lax.broadcasted_iota(jnp.int32, (sources, 128), 1) // HALF_FRAMES
        for s in range(4):
            tiles = [wide[pl.ds(4 * t + s, sources, stride=32), :] for t in range(8)]
            for bit in (1, 2, 4):
                shift = bit * HALF_FRAMES
                low = lane // bit % 2 == 0
                for t in range(8):
                    if t & bit == 0:
                        a, b = tiles[t], tiles[t + bit]
                        tiles[t] = jnp.where(low, a, pltpu.roll(b, shift, 1))
                        tiles[t + bit] = jnp.where(low, pltpu.roll(a, 128 - shift, 1), b)
            for p in range(GROUPS):
                for ri in range(2):
                    spectra[ri, pl.ds(p * 4 + s, sources, stride=INPUTS_HERE), :] = tiles[2 * p + ri]

    start = pl.multiple_of(step * ROWS, ROWS)
    real = spectra[0, pl.ds(start, ROWS), :].astype(BF16)
    imag = spectra[1, pl.ds(start, ROWS), :].astype(BF16)
    block = jnp.concatenate([real, imag], 1)
    swapped = jnp.concatenate([imag, -real], 1)
    everything = jnp.concatenate([spectra[0].astype(BF16), spectra[1].astype(BF16)], 1)
    contract = (((1,), (1,)), ((), ()))
    scale = 1.0 / 128
    out[0, 0] = (lax.dot_general(block, everything, contract, preferred_element_type=F32) * scale).astype(BF16)
    out[0, 1] = (lax.dot_general(swapped, everything, contract, preferred_element_type=F32) * scale).astype(BF16)


def correlate(arrived):
    inputs = arrived.shape[0] // 4 * INPUTS_HERE
    return pl.pallas_call(
        correlate_kernel,
        out_shape=jax.ShapeDtypeStruct((1, 2, inputs, inputs), BF16),
        grid=(inputs // ROWS,),
        in_specs=[pl.BlockSpec(arrived.shape, lambda i: (0, 0, 0))],
        out_specs=pl.BlockSpec((1, 2, ROWS, inputs), lambda i: (0, 0, i, 0)),
        scratch_shapes=[pltpu.VMEM((2, inputs, 128), F32), pltpu.VMEM((arrived.shape[0] * 8, 128), F32)],
        name="correlate",
    )(arrived)


def on_device(samples, coefficients):
    return correlate(gather_spectra(samples, coefficients))


def solution(mesh):
    return jax.shard_map(
        on_device,
        mesh=mesh,
        in_specs=(P("st", "ta", None), P()),
        out_specs=P(("st", "ta"), None, None, None),
        check_vma=False,
    )
```

time: 56.1 us -> 48.8 us (0.87)
  Pallas kernels: 55.9 us -> 48.6 us
    pallas_call x2 -> x1, Pallas kernels: 50.5 us -> 42.5 us  [gather_spectra(): pl.pallas_call(spectra_kernel, out_shape=jax.ShapeDtypeStruct((CHANNELS,...]
    pallas_call x1, Pallas kernels: 5.45 us -> 6.18 us  [correlate(): pl.pallas_call(correlate_kernel, out_shape=jax.ShapeDtypeStruct((1, 2, in...]
where the time goes in v2:
time: 48.8 us; the launch traced here: 48.6 us
  Pallas kernels  48.6 us (100%)
    pallas_call x1, Pallas kernels, gather_spectra(): pl.pallas_call(spectra_kernel, out_shape=jax.ShapeDtypeStruct((CHANNELS,...  42.5 us
    pallas_call x1, Pallas kernels, correlate(): pl.pallas_call(correlate_kernel, out_shape=jax.ShapeDtypeStruct((1, 2, in...  6.18 us

profile of v2, /device:TPU:1, one launch (start us, length us, event | category | flops | bytes accessed | tf_op | source)
XLA Modules:
  0.0 48.6 jit_solution(7125966298286647335)
XLA Ops:
  0.0 42.5 %spectra.1.arrived = bf16[256,8,128]{2,1,0:T(8,128)(2,1)} custom-call(bf16[512,8192]{1,0:T(8,128)(2,1)} %bitcast.1, bf16[512,8192]{1,0:T(8,128)(2,1)} %bitcast.2, bf16[512,8192]{1,0:T(8,128)(2,1)} %bitcast.3, bf16[512,8192]{1,0:T(8,128)(2,1)} %bitcast.4, f32[16,8192]{1,0:T(8,128)} %c3.1, f32[16,8192]{1,0:T(8,128)} %c3.1, f32[16,8192]{1,0:T(8,128)} %c3.1, ...), custom_call_target="tpu_custom_call" | custom-call | tf_op jit(solution)/shard_map/spectra/pallas_call | solution.py:249
  42.5 6.2 %correlate.1 = bf16[1,2,1024,1024]{3,2,1,0:T(8,128)(2,1)} custom-call(bf16[256,8,128]{2,1,0:T(8,128)(2,1)} %spectra.1.arrived), custom_call_target="tpu_custom_call" | custom-call | tf_op jit(solution)/shard_map/correlate/pallas_call | solution.py:320

commit v3 on v2

v3 whole, which is shorter than its diff:
```python
import functools
import math

import jax
import jax.numpy as jnp
import numpy as np
from jax import lax
from jax.experimental import pallas as pl
from jax.experimental.pallas import tpu as pltpu
from jax.sharding import PartitionSpec as P

CH0 = 1024
LOGICAL = pl.DeviceIdType.LOGICAL
BF16 = jnp.bfloat16
F32 = jnp.float32

NFFT = 8192
TAPS = 16
INPUTS_HERE = 16
FRAMES_HERE = 32
CHANNELS = 256
TA = 4
BINS = 24
HALF = 8
GROUPS = 4
HALF_FRAMES = FRAMES_HERE // 2
QUARTER = NFFT // 4
CHUNK = 256
STEPS = QUARTER // CHUNK


def _as_bf16(values):
    return np.asarray(values, np.float32).astype(BF16)


def _high_low(values):
    high = _as_bf16(values)
    return high, _as_bf16(values - high.astype(np.float64))


def _bin_angles():
    return 2.0 * np.pi * (np.arange(BINS) + 0.5) / (2 * BINS)


def _forward_matrix():
    angles = _bin_angles()[:, None] * np.arange(FRAMES_HERE)[None, :]
    parts = np.stack([np.cos(angles), -np.sin(angles)])
    block = np.zeros((HALF, 2, BINS, HALF, FRAMES_HERE))
    for i in range(HALF):
        block[i, :, :, i, :] = parts
    return block.reshape(2 * HALF * BINS, HALF * FRAMES_HERE)


def _tap_matrix():
    angles = _bin_angles()[:, None] * np.arange(TAPS)[None, :]
    taps = np.concatenate([np.cos(angles), np.sin(angles)])
    high, low = _high_low(taps)
    return np.concatenate([high, high, low], 1)


def _inverse_matrix():
    scale = (2.0 / (2 * BINS)) * NFFT ** -0.5
    rows = np.zeros((3, GROUPS, HALF_FRAMES, GROUPS, 2, BINS))
    for kind, first in enumerate((0, HALF_FRAMES, -HALF_FRAMES)):
        frames = first + np.arange(HALF_FRAMES)
        angles = _bin_angles()[:, None] * frames[None, :]
        values = scale * np.stack([np.cos(angles), -np.sin(angles)])
        if first < 0:
            values[:, :, frames <= -TAPS] = 0.0
        for p in range(GROUPS):
            rows[kind, p, :, p] = np.moveaxis(values, 2, 0)
    high, low = _high_low(rows.reshape(3 * GROUPS * HALF_FRAMES, 2 * GROUPS * BINS))
    return np.concatenate([high, high, low], 1)


def _channel_table():
    positions = np.arange(QUARTER)[:, None]
    columns = []
    for odd in range(2):
        channels = CH0 + np.arange(odd, CHANNELS, 2)[None, :]
        angles = 2.0 * np.pi * (positions * channels % NFFT) / NFFT
        columns += [np.cos(angles), -np.sin(angles)]
    return _as_bf16(np.concatenate(columns, 1))


def _turn_signs():
    even = np.where(np.arange(0, CHANNELS, 2) % 4 == 0, 1.0, -1.0)
    odd = np.where(np.arange(1, CHANNELS, 2) % 4 == 1, 1.0, -1.0)
    rows = np.concatenate([even, even, odd, -odd])[None, :]
    return _as_bf16(np.broadcast_to(rows, (16, 2 * CHANNELS)))


def _dot(a, b):
    return jnp.dot(a, b, preferred_element_type=F32)


def _split(values):
    high = values.astype(BF16)
    return high, (values - high.astype(F32)).astype(BF16)


def spectra_kernel(
    x, coefficients, table_all, inverse_all, signs, forward, taps,
    out,
    x_slots, c_slots, table_slots, inverse, in_sems, inverse_sem, acc, own, halo, early, late, leaving, arrived, wide, local_sem, halo_send, halo_recv, send_sem, recv_sem,
):
    step = pl.program_id(0)
    st = lax.axis_index("st")
    ta = lax.axis_index("ta")
    me = st * TA + ta
    barrier = pltpu.get_barrier_semaphore()

    def over_others(body):
        def run(peer, carry):
            body(peer)
            return carry

        lax.fori_loop(me + 1, CHANNELS, run, 0)
        lax.fori_loop(0, me, run, 0)

    def inputs(j):
        slot = lax.rem(j, 2)
        copies = []
        for q in range(4):
            columns = pl.ds(pl.multiple_of((q * STEPS + j) * CHUNK, CHUNK), CHUNK)
            copies.append(pltpu.make_async_copy(x.at[:, columns], x_slots.at[slot, q], in_sems.at[slot, q]))
            copies.append(
                pltpu.make_async_copy(coefficients.at[:, columns], c_slots.at[slot, q], in_sems.at[slot, 4 + q])
            )
        lines = pl.ds(pl.multiple_of(j * CHUNK, CHUNK), CHUNK)
        copies.append(pltpu.make_async_copy(table_all.at[lines], table_slots.at[slot], in_sems.at[slot, 8]))
        return copies

    inverse_copy = pltpu.make_async_copy(inverse_all, inverse, inverse_sem)

    @pl.when(step == 0)
    def _():
        for copy in inputs(step):
            copy.start()
        inverse_copy.start()
        over_others(lambda peer: pl.semaphore_signal(barrier, inc=1, device_id=peer, device_id_type=LOGICAL))
        acc[...] = jnp.zeros_like(acc)

    @pl.when(step < STEPS - 1)
    def _():
        for copy in inputs(step + 1):
            copy.start()

    for copy in inputs(step):
        copy.wait()
    slot = lax.rem(step, 2)
    table = table_slots[slot]
    tap_matrix = taps[...]
    responses = []
    for q in range(4):
        high, low = _split(c_slots[slot, q])
        response = _dot(tap_matrix, jnp.concatenate([high, low, high], 0))
        responses.append((response[:BINS][None], response[BINS:][None]))
    table_even = table[:, : CHANNELS]
    table_odd = table[:, CHANNELS :]
    half = CHANNELS // 2
    turned_even = table_even * signs[0:1, : CHANNELS]
    turned_odd = jnp.concatenate([table_odd[:, half:], table_odd[:, :half]], 1) * signs[0:1, CHANNELS :]
    matrix = forward[...]
    rows = HALF * FRAMES_HERE
    weights_even = jnp.concatenate([table_even, turned_even], 0)
    weights_odd = jnp.concatenate([table_odd, turned_odd], 0)

    def product(q, h):
        real, imag = responses[q]
        z = _dot(matrix, x_slots[slot, q, h * rows : (h + 1) * rows, :]).reshape(HALF, 2, BINS, CHUNK)
        zr, zi = z[:, 0], z[:, 1]
        return zr * real - zi * imag, zr * imag + zi * real

    def joined(r, i):
        return jnp.stack([r, i], 1).reshape(2 * HALF * BINS, CHUNK).astype(BF16)

    for h in range(2):
        evens, odds = [], []
        for q in range(2):
            (ra, ia), (rb, ib) = product(q, h), product(q + 2, h)
            evens.append(joined(ra + rb, ia + ib))
            odds.append(joined(ra - rb, ia - ib))
        acc[h, :, : CHANNELS] += _dot(jnp.concatenate(evens, 1), weights_even)
        acc[h, :, CHANNELS :] += _dot(jnp.concatenate(odds, 1), weights_odd)

    def transform_back():
        for s in range(HALF // 2):
            results = []
            for ri in range(2):
                left = ri * half
                blocks = []
                for p in range(GROUPS):
                    start = (p % 2 * 4 + s) * 2 * BINS
                    block = acc[p // 2, start : start + 2 * BINS, :]
                    blocks.append(
                        jnp.concatenate(
                            [block[:, left : left + half], block[:, CHANNELS + left : CHANNELS + left + half]], 1
                        )
                    )
                high, low = _split(jnp.concatenate(blocks, 0))
                results.append(_dot(inverse[...], jnp.concatenate([high, low, high], 0)))
            for odd in range(2):
                columns = slice(odd * half, (odd + 1) * half)

                def turned(kind):
                    lines = slice(kind * 64, (kind + 1) * 64)
                    return jnp.concatenate([results[0][lines, columns], results[1][lines, columns]], 0).T

                own[pl.ds(odd * 8 + s, half, stride=16), :] = turned(0)
                own[pl.ds(odd * 8 + 4 + s, half, stride=16), :] = turned(1)
                halo[pl.ds(odd * 4 + s, half, stride=8), :] = turned(2)

    def halo_copy(target):
        return pltpu.make_async_remote_copy(
            src_ref=leaving, dst_ref=arrived, send_sem=halo_send, recv_sem=halo_recv,
            device_id=st * TA + target, device_id_type=LOGICAL,
        )

    def part_copies(message, first):
        rows = pl.ds(first, 4)

        def send(peer):
            pltpu.make_async_remote_copy(
                src_ref=message.at[peer, rows], dst_ref=out.at[me, rows], send_sem=send_sem, recv_sem=recv_sem,
                device_id=peer, device_id_type=LOGICAL,
            ).start()

        keep = pltpu.make_async_copy(message.at[me, rows], out.at[me, rows], local_sem.at[first // 4])
        keep.start()
        over_others(send)
        return keep

    @pl.when(step == STEPS - 1)
    def _():
        inverse_copy.wait()
        transform_back()
        leaving[...] = halo[...].astype(BF16)
        early[...] = own[...].reshape(CHANNELS, HALF, 128).astype(BF16)
        pl.semaphore_wait(barrier, CHANNELS - 1)

        @pl.when(ta > 0)
        def _():
            halo_copy(ta - 1).start()

        keep_early = part_copies(early, 0)

        @pl.when(ta < TA - 1)
        def _():
            halo_copy(ta).wait_recv()
            wide[...] = arrived[...].astype(F32)
            for s in range(4):
                rows = pl.ds(4 + s, CHANNELS, stride=HALF)
                own[rows, :] += wide[pl.ds(s, CHANNELS, stride=4), :]

        late[...] = own[...].reshape(CHANNELS, HALF, 128).astype(BF16)
        keep_late = part_copies(late, 4)
        keep_early.wait()
        keep_late.wait()

        @pl.when(ta > 0)
        def _():
            halo_copy(ta - 1).wait_send()

        everything = pl.ds(0, CHANNELS - 1)
        pltpu.make_async_remote_copy(
            src_ref=late.at[everything], dst_ref=out.at[everything], send_sem=send_sem, recv_sem=recv_sem,
            device_id=me, device_id_type=LOGICAL,
        ).wait()


def gather_spectra(samples, coefficients):
    x = samples.reshape(INPUTS_HERE * FRAMES_HERE, NFFT)
    whole = lambda *shape: pl.BlockSpec(shape, lambda j: (0,) * len(shape))
    left = pl.BlockSpec(memory_space=pl.ANY)
    table, signs = _channel_table(), _turn_signs()
    forward, taps, inverse = _as_bf16(_forward_matrix()), _tap_matrix(), _inverse_matrix()
    rows = CHANNELS * HALF
    return pl.pallas_call(
        spectra_kernel,
        out_shape=jax.ShapeDtypeStruct((CHANNELS, HALF, 128), BF16),
        grid=(STEPS,),
        in_specs=[left, left, left, left, whole(*signs.shape), whole(*forward.shape), whole(*taps.shape)],
        out_specs=pl.BlockSpec(memory_space=pl.ANY),
        scratch_shapes=[
            pltpu.VMEM((2, 4, INPUTS_HERE * FRAMES_HERE, CHUNK), BF16),
            pltpu.VMEM((2, 4, TAPS, CHUNK), F32),
            pltpu.VMEM((2, CHUNK, 2 * CHANNELS), BF16),
            pltpu.VMEM(inverse.shape, BF16),
            pltpu.SemaphoreType.DMA((2, 9)),
            pltpu.SemaphoreType.DMA,
            pltpu.VMEM((2, 2 * HALF * BINS, 2 * CHANNELS), F32),
            pltpu.VMEM((rows, 128), F32),
            pltpu.VMEM((rows // 2, 128), F32),
            pltpu.VMEM((CHANNELS, HALF, 128), BF16),
            pltpu.VMEM((CHANNELS, HALF, 128), BF16),
            pltpu.VMEM((rows // 2, 128), BF16),
            pltpu.VMEM((rows // 2, 128), BF16),
            pltpu.VMEM((rows // 2, 128), F32),
            pltpu.SemaphoreType.DMA((2,)),
        ]
        + [pltpu.SemaphoreType.DMA] * 4,
        compiler_params=pltpu.CompilerParams(collective_id=0, has_side_effects=True),
        name="spectra",
    )(x, coefficients, table, inverse, signs, forward, taps)


ROWS = 256


def correlate_kernel(arrived, out, spectra, packed):
    stations = spectra.shape[1]
    step = pl.program_id(0)
    block = ROWS // INPUTS_HERE

    @pl.when(step == 0)
    def _():
        group = lax.broadcasted_iota(jnp.int32, (block, 8, 128), 2) // HALF_FRAMES

        def place(b, carry):
            start = pl.multiple_of(b * block, block)
            lines = arrived[pl.ds(start * TA, block * TA)].astype(F32).reshape(block, TA, 8, 128)
            tiles = [lines[:, t] for t in range(TA)]
            for bit in (1, 2):
                shift = bit * HALF_FRAMES
                low = group // bit % 2 == 0
                for t in range(TA):
                    if t & bit == 0:
                        first, second = tiles[t], tiles[t + bit]
                        tiles[t] = jnp.where(low, first, pltpu.roll(second, shift, 2))
                        tiles[t + bit] = jnp.where(low, pltpu.roll(first, 128 - shift, 2), second)
            for p in range(GROUPS):
                for late in range(2):
                    spectra[late, pl.ds(start, block), p * 4 : (p + 1) * 4, :] = tiles[p][:, late * 4 : late * 4 + 4]
            for late in range(2):
                rows = pl.ds(pl.multiple_of(b * ROWS, ROWS), ROWS)
                values = spectra[late, pl.ds(start, block)].reshape(ROWS, 128)
                packed[rows, late * 128 : (late + 1) * 128] = values.astype(BF16)
            return carry

        lax.fori_loop(0, stations // block, place, 0)

    here = pl.ds(pl.multiple_of(step * block, block), block)
    sign = jnp.where(lax.broadcasted_iota(jnp.int32, (1, 128), 1) < 64, 1.0, -1.0)
    direct, swapped = [], []
    for late in range(2):
        values = spectra[late, here].reshape(ROWS, 128)
        direct.append(values.astype(BF16))
        swapped.append((pltpu.roll(values, 64, 1) * sign).astype(BF16))
    lines = jnp.concatenate([jnp.concatenate(direct, 1), jnp.concatenate(swapped, 1)], 0)
    result = lax.dot_general(lines, packed[...], (((1,), (1,)), ((), ())), preferred_element_type=F32)
    scaled = (result * (1.0 / 128)).astype(BF16)
    out[0, 0] = scaled[:ROWS]
    out[0, 1] = scaled[ROWS:]


def correlate(arrived):
    inputs = arrived.shape[0] // TA * INPUTS_HERE
    return pl.pallas_call(
        correlate_kernel,
        out_shape=jax.ShapeDtypeStruct((1, 2, inputs, inputs), BF16),
        grid=(inputs // ROWS,),
        in_specs=[pl.BlockSpec(arrived.shape, lambda i: (0, 0, 0))],
        out_specs=pl.BlockSpec((1, 2, ROWS, inputs), lambda i: (0, 0, i, 0)),
        scratch_shapes=[
            pltpu.VMEM((2, inputs // INPUTS_HERE, INPUTS_HERE, 128), F32),
            pltpu.VMEM((inputs, 256), BF16),
        ],
        name="correlate",
    )(arrived)


def on_device(samples, coefficients):
    return correlate(gather_spectra(samples, coefficients))


def solution(mesh):
    return jax.shard_map(
        on_device,
        mesh=mesh,
        in_specs=(P("st", "ta", None), P()),
        out_specs=P(("st", "ta"), None, None, None),
        check_vma=False,
    )
```

time: 48.8 us -> 45.3 us (0.928)
  Pallas kernels: 48.6 us -> 45 us
    pallas_call x1, Pallas kernels: 42.5 us -> 39.6 us  [gather_spectra(): pl.pallas_call(spectra_kernel, out_shape=jax.ShapeDtypeStruct((CHANNELS,...]
    pallas_call x1, Pallas kernels: 6.18 us -> 5.36 us  [correlate(): pl.pallas_call(correlate_kernel, out_shape=jax.ShapeDtypeStruct((1, 2, in...]
where the time goes in v3:
time: 45.3 us; the launch traced here: 45 us
  Pallas kernels  45 us (99%)
    pallas_call x1, Pallas kernels, gather_spectra(): pl.pallas_call(spectra_kernel, out_shape=jax.ShapeDtypeStruct((CHANNELS,...  39.6 us
    pallas_call x1, Pallas kernels, correlate(): pl.pallas_call(correlate_kernel, out_shape=jax.ShapeDtypeStruct((1, 2, in...  5.36 us

profile of v3, /device:TPU:1, one launch (start us, length us, event | category | flops | bytes accessed | tf_op | source)
XLA Modules:
  0.0 45.0 jit_solution(5614416168048153613)
XLA Ops:
  0.0 39.6 %spectra.1.arrived = bf16[256,8,128]{2,1,0:T(8,128)(2,1)} custom-call(bf16[512,8192]{1,0:T(8,128)(2,1)} %bitcast.1, f32[16,8192]{1,0:T(8,128)} %coefficients.1, bf16[2048,512]{1,0:T(8,128)(2,1)} %constant.10.clone.table_all, bf16[192,576]{1,0:T(8,128)(2,1)} %constant.11.clone.inverse_all, bf16[16,512]{1,0:T(8,128)(2,1)} %constant.12.clone.signs, ...), custom_call_target="tpu_custom_call" | custom-call | tf_op jit(solution)/shard_map/spectra/pallas_call | solution.py:279
  39.6 5.4 %correlate.1 = bf16[1,2,1024,1024]{3,2,1,0:T(8,128)(2,1)} custom-call(bf16[256,8,128]{2,1,0:T(8,128)(2,1)} %spectra.1.arrived), custom_call_target="tpu_custom_call" | custom-call | tf_op jit(solution)/shard_map/correlate/pallas_call | solution.py:359

commit v4 on v3

--- a/solution.py
+++ b/solution.py
@@ -25,7 +25,7 @@
 GROUPS = 4
 HALF_FRAMES = FRAMES_HERE // 2
 QUARTER = NFFT // 4
-CHUNK = 256
+CHUNK = 512
 STEPS = QUARTER // CHUNK
 
 

time: 45.3 us -> 43.6 us (0.962)
  Pallas kernels: 45 us -> 43.5 us
    pallas_call x1, Pallas kernels: 39.6 us -> 38.1 us  [gather_spectra(): pl.pallas_call(spectra_kernel, out_shape=jax.ShapeDtypeStruct((CHANNELS,...]
where the time goes in v4:
time: 43.6 us; the launch traced here: 43.5 us
  Pallas kernels  43.5 us (100%)
    pallas_call x1, Pallas kernels, gather_spectra(): pl.pallas_call(spectra_kernel, out_shape=jax.ShapeDtypeStruct((CHANNELS,...  38.1 us
    pallas_call x1, Pallas kernels, correlate(): pl.pallas_call(correlate_kernel, out_shape=jax.ShapeDtypeStruct((1, 2, in...  5.36 us

profile of v4, /device:TPU:1, one launch (start us, length us, event | category | flops | bytes accessed | tf_op | source)
XLA Modules:
  0.0 43.5 jit_solution(6639274374757419256)
XLA Ops:
  0.0 38.1 %spectra.1.arrived = bf16[256,8,128]{2,1,0:T(8,128)(2,1)} custom-call(bf16[512,8192]{1,0:T(8,128)(2,1)} %bitcast.1, f32[16,8192]{1,0:T(8,128)} %coefficients.1, bf16[2048,512]{1,0:T(8,128)(2,1)} %constant.10.clone.table_all, bf16[192,576]{1,0:T(8,128)(2,1)} %constant.11.clone.inverse_all, bf16[16,512]{1,0:T(8,128)(2,1)} %constant.12.clone.signs, ...), custom_call_target="tpu_custom_call" | custom-call | tf_op jit(solution)/shard_map/spectra/pallas_call | solution.py:279
  38.1 5.4 %correlate.1 = bf16[1,2,1024,1024]{3,2,1,0:T(8,128)(2,1)} custom-call(bf16[256,8,128]{2,1,0:T(8,128)(2,1)} %spectra.1.arrived), custom_call_target="tpu_custom_call" | custom-call | tf_op jit(solution)/shard_map/correlate/pallas_call | solution.py:359

commit v5 on v4

--- a/solution.py
+++ b/solution.py
@@ -102,7 +102,7 @@
 def spectra_kernel(
     x, coefficients, table_all, inverse_all, signs, forward, taps,
     out,
-    x_slots, c_slots, table_slots, inverse, in_sems, inverse_sem, acc, own, halo, early, late, leaving, arrived, wide, local_sem, halo_send, halo_recv, send_sem, recv_sem,
+    x_slots, c_slots, table_slots, inverse, in_sems, inverse_sem, kept, kept_table, acc, own, halo, early, late, leaving, arrived, wide, local_sem, halo_send, halo_recv, send_sem, recv_sem,
 ):
     step = pl.program_id(0)
     st = lax.axis_index("st")
@@ -110,13 +110,9 @@
     me = st * TA + ta
     barrier = pltpu.get_barrier_semaphore()
 
-    def over_others(body):
-        def run(peer, carry):
-            body(peer)
-            return carry
-
-        lax.fori_loop(me + 1, CHANNELS, run, 0)
-        lax.fori_loop(0, me, run, 0)
+    def greet(peer, carry):
+        pl.semaphore_signal(barrier, inc=1, device_id=peer, device_id_type=LOGICAL)
+        return carry
 
     def inputs(j):
         slot = lax.rem(j, 2)
@@ -138,7 +134,8 @@
         for copy in inputs(step):
             copy.start()
         inverse_copy.start()
-        over_others(lambda peer: pl.semaphore_signal(barrier, inc=1, device_id=peer, device_id_type=LOGICAL))
+        lax.fori_loop(me + 1, CHANNELS, greet, 0)
+        lax.fori_loop(0, me, greet, 0)
         acc[...] = jnp.zeros_like(acc)
 
     @pl.when(step < STEPS - 1)
@@ -181,90 +178,119 @@
             (ra, ia), (rb, ib) = product(q, h), product(q + 2, h)
             evens.append(joined(ra + rb, ia + ib))
             odds.append(joined(ra - rb, ia - ib))
-        acc[h, :, : CHANNELS] += _dot(jnp.concatenate(evens, 1), weights_even)
-        acc[h, :, CHANNELS :] += _dot(jnp.concatenate(odds, 1), weights_odd)
-
-    def transform_back():
-        for s in range(HALF // 2):
+        acc[h] += _dot(jnp.concatenate(evens, 1), weights_even)
+        kept[h, :, pl.ds(pl.multiple_of(step * 2 * CHUNK, 2 * CHUNK), 2 * CHUNK)] = jnp.concatenate(odds, 1)
+
+    kept_table[pl.ds(pl.multiple_of(step * 2 * CHUNK, 2 * CHUNK), 2 * CHUNK), :] = weights_odd
+
+    def transform_back(parity):
+        for pair in range(2):
             results = []
             for ri in range(2):
-                left = ri * half
-                blocks = []
-                for p in range(GROUPS):
-                    start = (p % 2 * 4 + s) * 2 * BINS
-                    block = acc[p // 2, start : start + 2 * BINS, :]
-                    blocks.append(
-                        jnp.concatenate(
-                            [block[:, left : left + half], block[:, CHANNELS + left : CHANNELS + left + half]], 1
-                        )
-                    )
-                high, low = _split(jnp.concatenate(blocks, 0))
+                sides = []
+                for s in (2 * pair, 2 * pair + 1):
+                    blocks = []
+                    for p in range(GROUPS):
+                        start = (p % 2 * 4 + s) * 2 * BINS
+                        blocks.append(acc[p // 2, start : start + 2 * BINS, ri * half : (ri + 1) * half])
+                    sides.append(jnp.concatenate(blocks, 0))
+                high, low = _split(jnp.concatenate(sides, 1))
                 results.append(_dot(inverse[...], jnp.concatenate([high, low, high], 0)))
-            for odd in range(2):
-                columns = slice(odd * half, (odd + 1) * half)
+            for side in range(2):
+                s = 2 * pair + side
+                columns = slice(side * half, (side + 1) * half)
 
                 def turned(kind):
                     lines = slice(kind * 64, (kind + 1) * 64)
                     return jnp.concatenate([results[0][lines, columns], results[1][lines, columns]], 0).T
 
-                own[pl.ds(odd * 8 + s, half, stride=16), :] = turned(0)
-                own[pl.ds(odd * 8 + 4 + s, half, stride=16), :] = turned(1)
-                halo[pl.ds(odd * 4 + s, half, stride=8), :] = turned(2)
-
-    def halo_copy(target):
+                own[parity, pl.ds(s, half, stride=8), :] = turned(0)
+                own[parity, pl.ds(4 + s, half, stride=8), :] = turned(1)
+                halo[pl.ds(s, half, stride=4), :] = turned(2)
+        leaving[parity] = halo[...].astype(BF16)
+
+    def halo_copy(parity, target):
         return pltpu.make_async_remote_copy(
-            src_ref=leaving, dst_ref=arrived, send_sem=halo_send, recv_sem=halo_recv,
-            device_id=st * TA + target, device_id_type=LOGICAL,
+            src_ref=leaving.at[parity], dst_ref=arrived.at[parity], send_sem=halo_send.at[parity],
+            recv_sem=halo_recv.at[parity], device_id=st * TA + target, device_id_type=LOGICAL,
         )
 
-    def part_copies(message, first):
+    place = me // 2
+    other = [lax.rem(me, 2), 1 - lax.rem(me, 2)]
+
+    def keep_copy(message, parity, first):
         rows = pl.ds(first, 4)
-
-        def send(peer):
+        return pltpu.make_async_copy(message.at[parity, place, rows], out.at[me, rows], local_sem.at[first // 4])
+
+    def send_part(message, parity, first):
+        rows = pl.ds(first, 4)
+
+        def send(r, carry):
             pltpu.make_async_remote_copy(
-                src_ref=message.at[peer, rows], dst_ref=out.at[me, rows], send_sem=send_sem, recv_sem=recv_sem,
-                device_id=peer, device_id_type=LOGICAL,
+                src_ref=message.at[parity, r, rows], dst_ref=out.at[me, rows], send_sem=send_sem, recv_sem=recv_sem,
+                device_id=2 * r + parity, device_id_type=LOGICAL,
             ).start()
-
-        keep = pltpu.make_async_copy(message.at[me, rows], out.at[me, rows], local_sem.at[first // 4])
-        keep.start()
-        over_others(send)
-        return keep
+            return carry
+
+        @pl.when(other[parity] == 0)
+        def _():
+            keep_copy(message, parity, first).start()
+
+        lax.fori_loop(place + 1, half, send, 0)
+        lax.fori_loop(0, place + other[parity], send, 0)
+
+    def message_values(parity):
+        return own[parity].reshape(half, HALF, 128).astype(BF16)
+
+    def start_halo(parity):
+        @pl.when(ta > 0)
+        def _():
+            halo_copy(parity, ta - 1).start()
+
+    def add_halo(parity):
+        @pl.when(ta < TA - 1)
+        def _():
+            halo_copy(parity, ta).wait_recv()
+            wide[...] = arrived[parity].astype(F32)
+            for s in range(4):
+                rows = pl.ds(4 + s, half, stride=HALF)
+                own[parity, rows, :] += wide[pl.ds(s, half, stride=4), :]
 
     @pl.when(step == STEPS - 1)
     def _():
         inverse_copy.wait()
-        transform_back()
-        leaving[...] = halo[...].astype(BF16)
-        early[...] = own[...].reshape(CHANNELS, HALF, 128).astype(BF16)
+        transform_back(0)
         pl.semaphore_wait(barrier, CHANNELS - 1)
+        start_halo(0)
+        early[0] = message_values(0)
+        send_part(early, 0, 0)
+        for h in range(2):
+            acc[h] = _dot(kept[h], kept_table[...])
+        add_halo(0)
+        late[0] = message_values(0)
+        send_part(late, 0, 4)
+        transform_back(1)
+        start_halo(1)
+        early[1] = message_values(1)
+        send_part(early, 1, 0)
+        add_halo(1)
+        late[1] = message_values(1)
+        send_part(late, 1, 4)
+        for parity in range(2):
+
+            @pl.when(other[parity] == 0)
+            def _():
+                keep_copy(early, parity, 0).wait()
+                keep_copy(late, parity, 4).wait()
 
         @pl.when(ta > 0)
         def _():
-            halo_copy(ta - 1).start()
-
-        keep_early = part_copies(early, 0)
-
-        @pl.when(ta < TA - 1)
-        def _():
-            halo_copy(ta).wait_recv()
-            wide[...] = arrived[...].astype(F32)
-            for s in range(4):
-                rows = pl.ds(4 + s, CHANNELS, stride=HALF)
-                own[rows, :] += wide[pl.ds(s, CHANNELS, stride=4), :]
-
-        late[...] = own[...].reshape(CHANNELS, HALF, 128).astype(BF16)
-        keep_late = part_copies(late, 4)
-        keep_early.wait()
-        keep_late.wait()
-
-        @pl.when(ta > 0)
-        def _():
-            halo_copy(ta - 1).wait_send()
+            halo_copy(0, ta - 1).wait_send()
+            halo_copy(1, ta - 1).wait_send()
 
         everything = pl.ds(0, CHANNELS - 1)
         pltpu.make_async_remote_copy(
-            src_ref=late.at[everything], dst_ref=out.at[everything], send_sem=send_sem, recv_sem=recv_sem,
+            src_ref=out.at[everything], dst_ref=out.at[everything], send_sem=send_sem, recv_sem=recv_sem,
             device_id=me, device_id_type=LOGICAL,
         ).wait()
 
@@ -289,17 +315,19 @@
             pltpu.VMEM(inverse.shape, BF16),
             pltpu.SemaphoreType.DMA((2, 9)),
             pltpu.SemaphoreType.DMA,
-            pltpu.VMEM((2, 2 * HALF * BINS, 2 * CHANNELS), F32),
-            pltpu.VMEM((rows, 128), F32),
-            pltpu.VMEM((rows // 2, 128), F32),
-            pltpu.VMEM((CHANNELS, HALF, 128), BF16),
-            pltpu.VMEM((CHANNELS, HALF, 128), BF16),
-            pltpu.VMEM((rows // 2, 128), BF16),
-            pltpu.VMEM((rows // 2, 128), BF16),
-            pltpu.VMEM((rows // 2, 128), F32),
-            pltpu.SemaphoreType.DMA((2,)),
+            pltpu.VMEM((2, 2 * HALF * BINS, NFFT // 2), BF16),
+            pltpu.VMEM((NFFT // 2, CHANNELS), BF16),
+            pltpu.VMEM((2, 2 * HALF * BINS, CHANNELS), F32),
+            pltpu.VMEM((2, rows // 2, 128), F32),
+            pltpu.VMEM((rows // 4, 128), F32),
+            pltpu.VMEM((2, CHANNELS // 2, HALF, 128), BF16),
+            pltpu.VMEM((2, CHANNELS // 2, HALF, 128), BF16),
+            pltpu.VMEM((2, rows // 4, 128), BF16),
+            pltpu.VMEM((2, rows // 4, 128), BF16),
+            pltpu.VMEM((rows // 4, 128), F32),
         ]
-        + [pltpu.SemaphoreType.DMA] * 4,
+        + [pltpu.SemaphoreType.DMA((2,))] * 3
+        + [pltpu.SemaphoreType.DMA] * 2,
         compiler_params=pltpu.CompilerParams(collective_id=0, has_side_effects=True),
         name="spectra",
     )(x, coefficients, table, inverse, signs, forward, taps)
@@ -338,7 +366,7 @@
                 packed[rows, late * 128 : (late + 1) * 128] = values.astype(BF16)
             return carry
 
-        lax.fori_loop(0, stations // block, place, 0)
+        lax.fori_loop(0, stations // block, place, 0, unroll=4)
 
     here = pl.ds(pl.multiple_of(step * block, block), block)
     sign = jnp.where(lax.broadcasted_iota(jnp.int32, (1, 128), 1) < 64, 1.0, -1.0)

time: 43.6 us -> 42.8 us (0.982)
  Pallas kernels: 43.5 us -> 42.6 us
    pallas_call x1, Pallas kernels: 38.1 us -> 37.5 us  [gather_spectra(): pl.pallas_call(spectra_kernel, out_shape=jax.ShapeDtypeStruct((CHANNELS,...]
where the time goes in v5:
time: 42.8 us; the launch traced here: 42.7 us
  Pallas kernels  42.6 us (100%)
    pallas_call x1, Pallas kernels, gather_spectra(): pl.pallas_call(spectra_kernel, out_shape=jax.ShapeDtypeStruct((CHANNELS,...  37.5 us
    pallas_call x1, Pallas kernels, correlate(): pl.pallas_call(correlate_kernel, out_shape=jax.ShapeDtypeStruct((1, 2, in...  5.09 us

profile of v5, /device:TPU:1, one launch (start us, length us, event | category | flops | bytes accessed | tf_op | source)
XLA Modules:
  0.0 42.7 jit_solution(6119058723828498559)
XLA Ops:
  0.0 37.5 %spectra.1.arrived = bf16[256,8,128]{2,1,0:T(8,128)(2,1)} custom-call(bf16[512,8192]{1,0:T(8,128)(2,1)} %bitcast.1, f32[16,8192]{1,0:T(8,128)} %coefficients.1, bf16[2048,512]{1,0:T(8,128)(2,1)} %constant.10.clone.table_all, bf16[192,576]{1,0:T(8,128)(2,1)} %constant.11.clone.inverse_all, bf16[16,512]{1,0:T(8,128)(2,1)} %constant.12.clone.signs, ...), custom_call_target="tpu_custom_call" | custom-call | tf_op jit(solution)/shard_map/spectra/pallas_call | solution.py:305
  37.6 5.1 %correlate.1 = bf16[1,2,1024,1024]{3,2,1,0:T(8,128)(2,1)} custom-call(bf16[256,8,128]{2,1,0:T(8,128)(2,1)} %spectra.1.arrived), custom_call_target="tpu_custom_call" | custom-call | tf_op jit(solution)/shard_map/correlate/pallas_call | solution.py:387

commit v6 on v5

--- a/solution.py
+++ b/solution.py
@@ -333,7 +333,7 @@
     )(x, coefficients, table, inverse, signs, forward, taps)
 
 
-ROWS = 256
+ROWS = 128
 
 
 def correlate_kernel(arrived, out, spectra, packed):
@@ -366,7 +366,7 @@
                 packed[rows, late * 128 : (late + 1) * 128] = values.astype(BF16)
             return carry
 
-        lax.fori_loop(0, stations // block, place, 0, unroll=4)
+        lax.fori_loop(0, stations // block, place, 0, unroll=8)
 
     here = pl.ds(pl.multiple_of(step * block, block), block)
     sign = jnp.where(lax.broadcasted_iota(jnp.int32, (1, 128), 1) < 64, 1.0, -1.0)

time: 42.8 us -> 44.5 us (1.040)
  Pallas kernels: 42.6 us -> 44.3 us
    pallas_call x1, Pallas kernels: 5.09 us -> 6.77 us  [correlate(): pl.pallas_call(correlate_kernel, out_shape=jax.ShapeDtypeStruct((1, 2, in...]
where the time goes in v6:
time: 44.5 us; the launch traced here: 44.3 us
  Pallas kernels  44.3 us (100%)
    pallas_call x1, Pallas kernels, gather_spectra(): pl.pallas_call(spectra_kernel, out_shape=jax.ShapeDtypeStruct((CHANNELS,...  37.5 us
    pallas_call x1, Pallas kernels, correlate(): pl.pallas_call(correlate_kernel, out_shape=jax.ShapeDtypeStruct((1, 2, in...  6.77 us

profile of v6, /device:TPU:1, one launch (start us, length us, event | category | flops | bytes accessed | tf_op | source)
XLA Modules:
  0.0 44.3 jit_solution(9133409217852859561)
XLA Ops:
  0.0 37.5 %spectra.1.arrived = bf16[256,8,128]{2,1,0:T(8,128)(2,1)} custom-call(bf16[512,8192]{1,0:T(8,128)(2,1)} %bitcast.1, f32[16,8192]{1,0:T(8,128)} %coefficients.1, bf16[2048,512]{1,0:T(8,128)(2,1)} %constant.10.clone.table_all, bf16[192,576]{1,0:T(8,128)(2,1)} %constant.11.clone.inverse_all, bf16[16,512]{1,0:T(8,128)(2,1)} %constant.12.clone.signs, ...), custom_call_target="tpu_custom_call" | custom-call | tf_op jit(solution)/shard_map/spectra/pallas_call | solution.py:305
  37.6 6.8 %correlate.1 = bf16[1,2,1024,1024]{3,2,1,0:T(8,128)(2,1)} custom-call(bf16[256,8,128]{2,1,0:T(8,128)(2,1)} %spectra.1.arrived), custom_call_target="tpu_custom_call" | custom-call | tf_op jit(solution)/shard_map/correlate/pallas_call | solution.py:387
